TPU v7x, 32 devices: a whole 2x2x4 slice. The times are simulated.
32 devices in a mesh: dom: 32 (over z, y, x, core).
Axes of the slice: x: 2, y: 2, z: 4, core: 2. Of those that a mesh axis runs over, the one named last changes fastest.
Arguments:
- vectors: bfloat16 [64, 131072], P(None, 'dom')
- diag_tiles: bfloat16 [1024, 128, 128], P('dom'), as said below
- pair_tiles: bfloat16 [3072, 2, 128, 128], P('dom'), as said below
- halo_tiles: bfloat16 [1024, 128, 128], P('dom'), as said below
- halo_rows: int32 [32, 32], P('dom'), may hold values from 1 to 31, as said below
- pair_index: int32 [32, 96, 2], P('dom'), may hold values from 0 to 31, as said below
- pair_count: int32 [32], P('dom'), may hold values from 24 to 96, as said below
Outputs:
- basis: bfloat16 [64, 131072], P(None, 'dom')
- ritz: float32 [64, 64], replicated
Inputs may be any that keep to these rules, and one draw needn't show every extreme that they name: `diag_tiles`: each tile is symmetric. `pair_tiles`: entry [j, 1] is the transpose of entry [j, 0]. `halo_tiles`: entry d * 32 + p is the transpose of entry p * 32 + d. `halo_rows`: no entry is a multiple of 4. `pair_index`: the 96 entries of a partition are distinct pairs (r, c) with r < c. The first pair_count[d] entries of pair_index[d] are live; some partition has 96.
All inputs are finite; a program needn't handle non-finite values.
Results may differ from a plain program's by a relative error of at most 0.023.
Values may be sent and summed in bfloat16 or wider, within the bound.
A program may use at most 128 MiB of HBM per device.

v0:
```python
import jax
import jax.numpy as jnp
from jax import lax
from jax.sharding import PartitionSpec as P

DEGREE = 4


first_centre = -0.5


def local(vectors, diag_tiles, pair_tiles, halo_tiles, halo_rows, pair_index, pair_count):
    vec_width = vectors.shape[0]
    tile_size = diag_tiles.shape[1]
    blocks = diag_tiles.shape[0]
    peers = lax.axis_size("dom")
    total_rows = tile_size * blocks * peers
    block_iota = jnp.arange(blocks)
    row_ids = pair_index[0, :, 0]
    col_ids = pair_index[0, :, 1]
    live_mask = (jnp.arange(pair_index.shape[1]) < pair_count[0]).astype(jnp.float32)
    onehot_first = (row_ids[:, None] == block_iota[None, :]).astype(jnp.float32) * live_mask[
        :, None
    ]
    onehot_second = (col_ids[:, None] == block_iota[None, :]).astype(jnp.float32) * live_mask[
        :, None
    ]
    send_rows = halo_rows[0]
    onehot_halo = (send_rows[:, None] == block_iota[None, :]).astype(jnp.float32)

    def halo_terms(arrived):
        products = jnp.einsum(
            "kpj,pij->kpi", arrived, halo_tiles, preferred_element_type=jnp.float32
        )
        return jnp.einsum("kpi,pr->kri", products, onehot_halo)

    def operator(current):
        blocked = current.reshape(vec_width, blocks, tile_size)
        outgoing = jnp.take(blocked, send_rows, axis=1)
        result = halo_terms(
            lax.all_to_all(outgoing, "dom", split_axis=1, concat_axis=1, tiled=True)
        )
        result = result + jnp.einsum(
            "krj,rij->kri", blocked, diag_tiles, preferred_element_type=jnp.float32
        )
        from_cols = jnp.take(blocked, col_ids, axis=1)
        from_rows = jnp.take(blocked, row_ids, axis=1)
        upper_terms = jnp.einsum(
            "kej,eij->kei", from_cols, pair_tiles[:, 0], preferred_element_type=jnp.float32
        )
        lower_terms = jnp.einsum(
            "kej,eji->kei", from_rows, pair_tiles[:, 0], preferred_element_type=jnp.float32
        )
        result = result + jnp.einsum("kei,er->kri", upper_terms, onehot_first)
        result = result + jnp.einsum("kei,er->kri", lower_terms, onehot_second)
        return result.reshape(vec_width, blocks * tile_size)

    def subspace_step(start, first, centre):
        previous = start
        current = (first - centre * start.astype(jnp.float32)).astype(jnp.bfloat16)
        for degree in range(DEGREE - 1):
            applied = operator(current)
            following = (
                2.0 * (applied - centre * current.astype(jnp.float32))
                - previous.astype(jnp.float32)
            ).astype(jnp.bfloat16)
            previous, current = (current, following)
        partial_value = jnp.dot(current, current.T, preferred_element_type=jnp.float32) / total_rows
        gram_matrix = lax.psum(partial_value, "dom")
        chol_lower = jnp.linalg.cholesky(gram_matrix)
        inverse = jax.scipy.linalg.solve_triangular(
            chol_lower, jnp.eye(vec_width, dtype=jnp.float32), lower=True
        )
        following = jnp.dot(
            inverse, current.astype(jnp.float32), precision=lax.Precision.HIGHEST
        ).astype(jnp.bfloat16)
        applied = operator(following)
        projected = (
            jnp.dot(following.astype(jnp.float32), applied.T, precision=lax.Precision.HIGHEST)
            / total_rows
        )
        return (following, applied, projected)

    first = operator(vectors)
    basis_one, image_one, partial_one = subspace_step(vectors, first, first_centre)
    mean_ritz = jnp.trace(lax.psum(partial_one, "dom")) / vec_width
    basis, image_two, partial_two = subspace_step(basis_one, image_one, mean_ritz - 1.0)
    ritz = lax.psum(partial_two, "dom")
    return (basis, ritz)


def solution(mesh):
    return jax.shard_map(
        local,
        mesh=mesh,
        in_specs=(
            P(None, "dom"),
            P("dom", None, None),
            P("dom", None, None, None),
            P("dom", None, None),
            P("dom", None),
            P("dom", None, None),
            P("dom"),
        ),
        out_specs=(P(None, "dom"), P()),
        check_vma=False,
    )
```

profile of v0, /device:TPU:0, one launch (start us, length us, event | category | flops | bytes accessed | tf_op | source)
XLA Modules:
  0.0 501.4 jit_solution(12377639445538355991)
XLA Ops:
  4.8 7.3 %all-to-all-start = ((bf16[64,32,128]{2,0,1:T(8,128)(2,1)}), bf16[64,32,128]{2,0,1:T(8,128)(2,1)S(1)}, u32[]{:S(2)}, u32[]{:S(2)}) async-start(bf16[64,32,128]{2,0,1:T(8,128)(2,1)} %select_bitcast_fusion.8), calls=%async_computation | async-start | bytes 1048576 | tf_op jit(solution)/shard_map/all_to_all | solution.py:41
  14.8 4.6 fusion.75
  25.2 5.4 %fusion.72 = bf16[64,96,128]{2,0,1:T(8,128)(2,1)} fusion(bf16[96,64,128]{2,1,0:T(8,128)(2,1)S(1)} %copy-done.59, pred[96]{0:T(512)(128)(4,1)S(1)} %get-tuple-element.12, bf16[96,2,128,128]{3,2,1,0:T(8,128)(2,1)} %param.16), kind=kOutput, calls=%fused_computation.101 | convolution fusion | flops 202113024 | bytes 6291552 | tf_op jit(solution)/shard_map/kej,eij->kei/dot_general | solution.py:48
  40.6 6.4 %all-to-all-start.1 = ((bf16[64,32,128]{2,0,1:T(8,128)(2,1)}), bf16[64,32,128]{2,0,1:T(8,128)(2,1)}, u32[]{:S(2)}, u32[]{:S(2)}) async-start(bf16[64,32,128]{2,0,1:T(8,128)(2,1)} %select_bitcast_fusion.7), calls=%async_computation.1 | async-start | bytes 1048576 | tf_op jit(solution)/shard_map/all_to_all | solution.py:41
  57.4 5.3 %fusion.78 = bf16[64,96,128]{2,0,1:T(8,128)(2,1)} fusion(bf16[96,64,128]{2,1,0:T(8,128)(2,1)S(1)} %copy-done.60, pred[96]{0:T(512)(128)(4,1)S(1)} %get-tuple-element.12, bf16[96,2,128,128]{3,2,1,0:T(8,128)(2,1)} %param.16), kind=kOutput, calls=%fused_computation.103 | convolution fusion | flops 202113024 | bytes 6291552 | tf_op jit(solution)/shard_map/kej,eij->kei/dot_general | solution.py:48
  74.8 6.2 %all-to-all-start.2 = ((bf16[64,32,128]{2,0,1:T(8,128)(2,1)}), bf16[64,32,128]{2,0,1:T(8,128)(2,1)}, u32[]{:S(2)}, u32[]{:S(2)}) async-start(bf16[64,32,128]{2,0,1:T(8,128)(2,1)} %select_bitcast_fusion.6), calls=%async_computation.2 | async-start | bytes 1048576 | tf_op jit(solution)/shard_map/all_to_all | solution.py:41
  92.6 5.3 %fusion.84 = bf16[64,96,128]{2,0,1:T(8,128)(2,1)} fusion(bf16[96,64,128]{2,1,0:T(8,128)(2,1)S(1)} %copy-done.61, pred[96]{0:T(512)(128)(4,1)S(1)} %get-tuple-element.12, bf16[96,2,128,128]{3,2,1,0:T(8,128)(2,1)} %param.16), kind=kOutput, calls=%fused_computation.105 | convolution fusion | flops 202113024 | bytes 6291552 | tf_op jit(solution)/shard_map/kej,eij->kei/dot_general | solution.py:48
  111.7 6.3 %all-to-all-start.3 = ((bf16[64,32,128]{2,0,1:T(8,128)(2,1)}), bf16[64,32,128]{2,0,1:T(8,128)(2,1)}, u32[]{:S(2)}, u32[]{:S(2)}) async-start(bf16[64,32,128]{2,0,1:T(8,128)(2,1)} %select_bitcast_fusion.5), calls=%async_computation.3 | async-start | bytes 1048576 | tf_op jit(solution)/shard_map/all_to_all | solution.py:41
  125.4 5.3 %fusion.90 = bf16[64,96,128]{2,0,1:T(8,128)(2,1)} fusion(bf16[96,64,128]{2,1,0:T(8,128)(2,1)S(1)} %copy-done.56, pred[96]{0:T(512)(128)(4,1)S(1)} %get-tuple-element.12, bf16[96,2,128,128]{3,2,1,0:T(8,128)(2,1)} %param.16), kind=kOutput, calls=%fused_computation.107 | convolution fusion | flops 202113024 | bytes 6291552 | tf_op jit(solution)/shard_map/kej,eij->kei/dot_general | solution.py:48
  141.5 39.4 %psum.28 = f32[64,64]{0,1:T(8,128)S(1)} all-reduce(f32[64,64]{0,1:T(8,128)S(1)} %convolution_multiply_fusion.3), channel_id=1, replica_groups=mesh['dom'=32] {'dom'}, use_global_device_ids=true, to_apply=%region_0.3 | all-reduce | flops 4096 | bytes 32768 | tf_op jit(solution)/shard_map/psum | solution.py:69
  181.0 5.8 %cholesky.44 = f32[64,64]{1,0:T(8,128)S(1)} custom-call(f32[64,64]{1,0:T(8,128)S(1)} %fusion.301), custom_call_target="Cholesky" | custom-call | tf_op jit(solution)/shard_map/jit(cholesky)/cholesky | solution.py:70
  188.2 4.9 custom-call.6
  214.8 5.3 %fusion.96 = bf16[64,96,128]{2,0,1:T(8,128)(2,1)} fusion(bf16[96,64,128]{2,1,0:T(8,128)(2,1)S(1)} %copy-done.62, pred[96]{0:T(512)(128)(4,1)S(1)} %get-tuple-element.12, bf16[96,2,128,128]{3,2,1,0:T(8,128)(2,1)} %param.16), kind=kOutput, calls=%fused_computation.109 | convolution fusion | flops 202113024 | bytes 6291552 | tf_op jit(solution)/shard_map/kej,eij->kei/dot_general | solution.py:48
  227.2 40.7 %psum.29 = f32[64,64]{0,1:T(8,128)S(1)} all-reduce(f32[64,64]{0,1:T(8,128)S(1)} %convolution_multiply_fusion.2), channel_id=1, replica_groups=mesh['dom'=32] {'dom'}, use_global_device_ids=true, to_apply=%region_3.8 | all-reduce | flops 4096 | bytes 32768 | tf_op jit(solution)/shard_map/psum | solution.py:86
  291.5 5.3 %fusion.102 = bf16[64,96,128]{2,0,1:T(8,128)(2,1)} fusion(bf16[96,64,128]{2,1,0:T(8,128)(2,1)S(1)} %copy-done.63, pred[96]{0:T(512)(128)(4,1)S(1)} %get-tuple-element.12, bf16[96,2,128,128]{3,2,1,0:T(8,128)(2,1)} %param.16), kind=kOutput, calls=%fused_computation.111 | convolution fusion | flops 202113024 | bytes 6291552 | tf_op jit(solution)/shard_map/kej,eij->kei/dot_general | solution.py:48
  308.8 6.1 %all-to-all-start.6 = ((bf16[64,32,128]{2,0,1:T(8,128)(2,1)}), bf16[64,32,128]{2,0,1:T(8,128)(2,1)}, u32[]{:S(2)}, u32[]{:S(2)}) async-start(bf16[64,32,128]{2,0,1:T(8,128)(2,1)} %select_bitcast_fusion.2), calls=%async_computation.6 | async-start | bytes 1048576 | tf_op jit(solution)/shard_map/all_to_all | solution.py:41
  326.5 5.3 %fusion.108 = bf16[64,96,128]{2,0,1:T(8,128)(2,1)} fusion(bf16[96,64,128]{2,1,0:T(8,128)(2,1)S(1)} %copy-done.64, pred[96]{0:T(512)(128)(4,1)S(1)} %get-tuple-element.12, bf16[96,2,128,128]{3,2,1,0:T(8,128)(2,1)} %param.16), kind=kOutput, calls=%fused_computation.113 | convolution fusion | flops 202113024 | bytes 6291552 | tf_op jit(solution)/shard_map/kej,eij->kei/dot_general | solution.py:48
  345.6 6.5 %all-to-all-start.7 = ((bf16[64,32,128]{2,0,1:T(8,128)(2,1)}), bf16[64,32,128]{2,0,1:T(8,128)(2,1)}, u32[]{:S(2)}, u32[]{:S(2)}) async-start(bf16[64,32,128]{2,0,1:T(8,128)(2,1)} %select_bitcast_fusion.1), calls=%async_computation.7 | async-start | bytes 1048576 | tf_op jit(solution)/shard_map/all_to_all | solution.py:41
  359.5 5.3 %fusion.114 = bf16[64,96,128]{2,0,1:T(8,128)(2,1)} fusion(bf16[96,64,128]{2,1,0:T(8,128)(2,1)S(1)} %copy-done.57, pred[96]{0:T(512)(128)(4,1)S(1)} %get-tuple-element.12, bf16[96,2,128,128]{3,2,1,0:T(8,128)(2,1)} %param.16), kind=kOutput, calls=%fused_computation.115 | convolution fusion | flops 202113024 | bytes 6291552 | tf_op jit(solution)/shard_map/kej,eij->kei/dot_general | solution.py:48
  375.5 39.2 %psum.30 = f32[64,64]{0,1:T(8,128)S(1)} all-reduce(f32[64,64]{0,1:T(8,128)S(1)} %convolution_multiply_fusion.1), channel_id=1, replica_groups=mesh['dom'=32] {'dom'}, use_global_device_ids=true, to_apply=%region_5.10 | all-reduce | flops 4096 | bytes 32768 | tf_op jit(solution)/shard_map/psum | solution.py:69
  414.8 5.8 %cholesky.55 = f32[64,64]{1,0:T(8,128)S(1)} custom-call(f32[64,64]{1,0:T(8,128)S(1)} %fusion.299), custom_call_target="Cholesky" | custom-call | tf_op jit(solution)/shard_map/jit(cholesky)/cholesky | solution.py:70
  422.0 4.9 custom-call.7
  448.6 5.3 %fusion.120 = bf16[64,96,128]{2,0,1:T(8,128)(2,1)} fusion(bf16[96,64,128]{2,1,0:T(8,128)(2,1)S(1)} %copy-done.58, pred[96]{0:T(512)(128)(4,1)S(1)} %get-tuple-element.12, bf16[96,2,128,128]{3,2,1,0:T(8,128)(2,1)} %param.16), kind=kOutput, calls=%fused_computation.117 | convolution fusion | flops 202113024 | bytes 6291552 | tf_op jit(solution)/shard_map/kej,eij->kei/dot_general | solution.py:48
  460.0 40.5 %psum.31 = f32[64,64]{0,1:T(8,128)S(1)} all-reduce(f32[64,64]{0,1:T(8,128)S(1)} %convolution_multiply_fusion), channel_id=1, replica_groups=mesh['dom'=32] {'dom'}, use_global_device_ids=true, to_apply=%region_6.11 | all-reduce | flops 4096 | bytes 32768 | tf_op jit(solution)/shard_map/psum | solution.py:88
  (277 shorter events, 225.5 us)
Async XLA Ops:
  0.6 20.7 %copy-start = (bf16[32,128,128]{2,1,0:T(8,128)(2,1)S(1)}, bf16[32,128,128]{2,1,0:T(8,128)(2,1)}, u32[]{:S(2)}) copy-start(bf16[32,128,128]{2,1,0:T(8,128)(2,1)} %param.15) | copy-start | bytes 3145732
  3.3 8.9 %copy-start.66 = (s32[1,96,2]{1,2,0:T(2,128)S(1)}, s32[1,96,2]{1,2,0:T(2,128)}, u32[]{:S(2)}) copy-start(s32[1,96,2]{1,2,0:T(2,128)} %param.19) | copy-start | bytes 2308
  4.8 25.8 %all-to-all-start = ((bf16[64,32,128]{2,0,1:T(8,128)(2,1)}), bf16[64,32,128]{2,0,1:T(8,128)(2,1)S(1)}, u32[]{:S(2)}, u32[]{:S(2)}) async-start(bf16[64,32,128]{2,0,1:T(8,128)(2,1)} %select_bitcast_fusion.8), calls=%async_computation | async-start | bytes 1048576 | tf_op jit(solution)/shard_map/all_to_all | solution.py:41
  23.1 2.1 copy-start.59
  25.2 5.4 %copy-start.1 = (bf16[32,128,128]{2,1,0:T(8,128)(2,1)S(1)}, bf16[32,128,128]{2,1,0:T(8,128)(2,1)}, u32[]{:S(2)}) copy-start(bf16[32,128,128]{2,1,0:T(8,128)(2,1)} %param.17) | copy-start | bytes 3145732
  40.6 22.2 %all-to-all-start.1 = ((bf16[64,32,128]{2,0,1:T(8,128)(2,1)}), bf16[64,32,128]{2,0,1:T(8,128)(2,1)}, u32[]{:S(2)}, u32[]{:S(2)}) async-start(bf16[64,32,128]{2,0,1:T(8,128)(2,1)} %select_bitcast_fusion.7), calls=%async_computation.1 | async-start | bytes 1048576 | tf_op jit(solution)/shard_map/all_to_all | solution.py:41
  55.3 2.1 copy-start.60
  74.8 23.1 %all-to-all-start.2 = ((bf16[64,32,128]{2,0,1:T(8,128)(2,1)}), bf16[64,32,128]{2,0,1:T(8,128)(2,1)}, u32[]{:S(2)}, u32[]{:S(2)}) async-start(bf16[64,32,128]{2,0,1:T(8,128)(2,1)} %select_bitcast_fusion.6), calls=%async_computation.2 | async-start | bytes 1048576 | tf_op jit(solution)/shard_map/all_to_all | solution.py:41
  87.5 3.0 copy-start.52
  101.6 2.1 copy-start.5
  111.7 21.9 %all-to-all-start.3 = ((bf16[64,32,128]{2,0,1:T(8,128)(2,1)}), bf16[64,32,128]{2,0,1:T(8,128)(2,1)}, u32[]{:S(2)}, u32[]{:S(2)}) async-start(bf16[64,32,128]{2,0,1:T(8,128)(2,1)} %select_bitcast_fusion.5), calls=%async_computation.3 | async-start | bytes 1048576 | tf_op jit(solution)/shard_map/all_to_all | solution.py:41
  121.4 2.1 copy-start.6
  121.4 2.1 copy-start.14
  195.0 74.2 %copy-start.2 = (bf16[64,4096]{1,0:T(8,128)(2,1)}, bf16[64,4096]{1,0:T(8,128)(2,1)S(1)}, u32[]{:S(2)}) copy-start(bf16[64,4096]{1,0:T(8,128)(2,1)S(1)} %convolution_convert_fusion.1) | copy-start | bytes 1572868
  200.5 19.6 %all-to-all-start.4 = ((bf16[64,32,128]{2,0,1:T(8,128)(2,1)}), bf16[64,32,128]{2,0,1:T(8,128)(2,1)}, u32[]{:S(2)}, u32[]{:S(2)}) async-start(bf16[64,32,128]{2,0,1:T(8,128)(2,1)} %select_bitcast_fusion.4), calls=%async_computation.4 | async-start | bytes 1048576 | tf_op jit(solution)/shard_map/all_to_all | solution.py:41
  276.5 20.3 %all-to-all-start.5 = ((bf16[64,32,128]{2,0,1:T(8,128)(2,1)}), bf16[64,32,128]{2,0,1:T(8,128)(2,1)}, u32[]{:S(2)}, u32[]{:S(2)}) async-start(bf16[64,32,128]{2,0,1:T(8,128)(2,1)} %select_bitcast_fusion.3), calls=%async_computation.5 | async-start | bytes 1048576 | tf_op jit(solution)/shard_map/all_to_all | solution.py:41
  308.8 23.0 %all-to-all-start.6 = ((bf16[64,32,128]{2,0,1:T(8,128)(2,1)}), bf16[64,32,128]{2,0,1:T(8,128)(2,1)}, u32[]{:S(2)}, u32[]{:S(2)}) async-start(bf16[64,32,128]{2,0,1:T(8,128)(2,1)} %select_bitcast_fusion.2), calls=%async_computation.6 | async-start | bytes 1048576 | tf_op jit(solution)/shard_map/all_to_all | solution.py:41
  321.4 3.0 copy-start.55
  335.5 2.1 copy-start.8
  345.6 22.1 %all-to-all-start.7 = ((bf16[64,32,128]{2,0,1:T(8,128)(2,1)}), bf16[64,32,128]{2,0,1:T(8,128)(2,1)}, u32[]{:S(2)}, u32[]{:S(2)}) async-start(bf16[64,32,128]{2,0,1:T(8,128)(2,1)} %select_bitcast_fusion.1), calls=%async_computation.7 | async-start | bytes 1048576 | tf_op jit(solution)/shard_map/all_to_all | solution.py:41
  355.5 2.1 copy-start.9
  355.5 2.1 copy-start.11
  428.8 30.0 %copy-start.17 = (bf16[64,4096]{1,0:T(8,128)(2,1)}, bf16[64,4096]{1,0:T(8,128)(2,1)S(1)}, u32[]{:S(2)}) copy-start(bf16[64,4096]{1,0:T(8,128)(2,1)S(1)} %convolution_convert_fusion) | copy-start | bytes 1572868
  434.3 19.6 %all-to-all-start.8 = ((bf16[64,32,128]{2,0,1:T(8,128)(2,1)}), bf16[64,32,128]{2,0,1:T(8,128)(2,1)}, u32[]{:S(2)}, u32[]{:S(2)}) async-start(bf16[64,32,128]{2,0,1:T(8,128)(2,1)} %select_bitcast_fusion), calls=%async_computation.8 | async-start | bytes 1048576 | tf_op jit(solution)/shard_map/all_to_all | solution.py:41
  (52 other events, 80.4 us)
where the time goes:
time: 510 us; the launch traced here: 501 us
  matrix products  165 us (32%)
  blocking collectives  160 us (31%)
  local copies, waits for them, and re-layouts  63.9 us (13%)
  other arithmetic  52.2 us (10%)
  starting transfers between devices  51.3 us (10%)
  waiting for transfers between devices  5.72 us (1%)
    psum x2, blocking collectives, subspace_step(): gram_matrix = lax.psum(partial_value, 'dom')  78.6 us
    all_to_all x9, starting transfers between devices, operator(): lax.all_to_all(outgoing, 'dom', split_axis=1, concat_axis=1, tiled=True)  51.3 us
    dot_general x9, matrix products, operator(): jnp.einsum('kej,eij->kei', from_cols, pair_tiles[:, 0], preferred_element...  48 us
    psum x1, blocking collectives, local(): mean_ritz = jnp.trace(lax.psum(partial_one, 'dom')) / vec_width  40.7 us
    psum x1, blocking collectives, local(): ritz = lax.psum(partial_two, 'dom')  40.5 us
    dot_general x9, matrix products, operator(): jnp.einsum('kej,eji->kei', from_rows, pair_tiles[:, 0], preferred_element...  38.6 us
    dot_general x9, matrix products, operator(): result = result + jnp.einsum('kei,er->kri', lower_terms, onehot_second)  18.7 us
    dot_general x9, matrix products, operator(): jnp.einsum('krj,rij->kri', blocked, diag_tiles, preferred_element_type=jn...  18.6 us
  transfers between devices with their start and end apart: 9, of which 2 were waited for; matrix products, arithmetic and copies ran while one was open for 28% of the time, Pallas kernels for 0%

commit v1 on v0

v1 whole, which is shorter than its diff:
```python
import functools

import jax
import jax.numpy as jnp
from jax import lax
from jax.experimental import pallas as pl
from jax.experimental.pallas import tpu as pltpu
from jax.sharding import PartitionSpec as P

DEGREE = 4
FIRST_CENTRE = -0.5
MESH = pl.DeviceIdType.MESH
f32 = jnp.float32
bf16 = jnp.bfloat16


def nt_dot(a, b):
    return lax.dot_general(a, b, (((1,), (1,)), ((), ())), preferred_element_type=f32)


def kernel(
    n,
    total_rows,
    tile_id,
    source_id,
    keep,
    end_of,
    send_rows,
    halo_order,
    halo_keep,
    halo_end,
    halo_any,
    vec_ref,
    diag_hbm,
    pair_hbm,
    halo_hbm,
    basis_ref,
    ritz_ref,
    tiles,
    halo_tiles,
    y_buf,
    image,
    partial,
    halo_part,
    stage,
    arrived_even,
    arrived_odd,
    red_out,
    red_in,
    load_sem,
    send_sem,
    recv_sem,
    red_send,
    red_recv,
):
    me = lax.axis_index("dom")
    k, width = vec_ref.shape
    blocks = y_buf.shape[1]
    b = width // blocks
    entries = tiles.shape[0]
    pairs2 = entries - blocks

    loads = [
        pltpu.make_async_copy(diag_hbm, tiles.at[pl.ds(0, blocks)], load_sem.at[0]),
        pltpu.make_async_copy(pair_hbm, tiles.at[pl.ds(blocks, pairs2)], load_sem.at[1]),
        pltpu.make_async_copy(halo_hbm, halo_tiles, load_sem.at[2]),
    ]
    for load in loads:
        load.start()

    barrier = pltpu.get_barrier_semaphore()

    def greet(s, _):
        pl.semaphore_signal(
            barrier, inc=1, device_id=(lax.rem(me + s, n),), device_id_type=MESH
        )
        return 0

    lax.fori_loop(1, n, greet, 0)
    for j in range(blocks):
        y_buf[0, j] = vec_ref[:, j * b : (j + 1) * b]
    pl.semaphore_wait(barrier, n - 1)

    slots = (arrived_even, arrived_odd)

    def halo_copy(slot, peer_from, peer_to):
        return pltpu.make_async_remote_copy(
            src_ref=stage.at[peer_to],
            dst_ref=slots[slot].at[peer_from],
            send_sem=send_sem.at[peer_to],
            recv_sem=recv_sem.at[slot, peer_from],
            device_id=(peer_to,),
            device_id_type=MESH,
        )

    entry_unroll = next(u for u in (8, 4, 2, 1) if entries % u == 0)
    halo_unroll = next(u for u in (8, 4, 2, 1) if n % u == 0)

    def operator(count, cur):
        slot = count % 2
        arrived = slots[slot]

        def send(s, _):
            peer = lax.rem(me + s, n)
            stage[peer] = y_buf[cur, send_rows[peer]]
            halo_copy(slot, me, peer).start()
            return 0

        lax.fori_loop(1, n, send, 0)
        arrived[me] = y_buf[cur, send_rows[me]]
        if count == 0:
            for load in loads:
                load.wait()

        def local(i, carry):
            for u in range(entry_unroll):
                e = i * entry_unroll + u
                product = jnp.dot(
                    y_buf[cur, source_id[e]], tiles[tile_id[e]], preferred_element_type=f32
                )
                carry = carry * keep[e] + product
                partial[e] = carry
            return carry

        lax.fori_loop(0, entries // entry_unroll, local, jnp.zeros((k, b), f32))

        def receive(s, _):
            peer = lax.rem(me + n - s, n)
            halo_copy(slot, peer, peer).wait_recv()
            return 0

        lax.fori_loop(1, n, receive, 0)

        def halo(i, carry):
            for u in range(halo_unroll):
                e = i * halo_unroll + u
                p = halo_order[e]
                carry = carry * halo_keep[e] + nt_dot(arrived[p], halo_tiles[p])
                halo_part[e] = carry
            return carry

        lax.fori_loop(0, n // halo_unroll, halo, jnp.zeros((k, b), f32))

        def sent(s, _):
            halo_copy(slot, me, lax.rem(me + s, n)).wait_send()
            return 0

        lax.fori_loop(1, n, sent, 0)

    def applied(r):
        return partial[end_of[r]] + halo_part[halo_end[r]] * halo_any[r]

    def over_blocks(body, init, unroll=4):
        def step(i, carry):
            for u in range(unroll):
                carry = body(i * unroll + u, carry)
            return carry

        if blocks % unroll:
            return lax.fori_loop(0, blocks, body, init)
        return lax.fori_loop(0, blocks // unroll, step, init)

    def reduce_sum(value):
        rows = value.shape[0]
        red_out[0:rows] = value
        red_in[me, 0:rows] = value

        def copy(peer_from, peer_to):
            return pltpu.make_async_remote_copy(
                src_ref=red_out.at[pl.ds(0, rows)],
                dst_ref=red_in.at[peer_from, pl.ds(0, rows)],
                send_sem=red_send.at[peer_to],
                recv_sem=red_recv.at[peer_from],
                device_id=(peer_to,),
                device_id_type=MESH,
            )

        def send(s, _):
            copy(me, lax.rem(me + s, n)).start()
            return 0

        def receive(s, _):
            peer = lax.rem(me + n - s, n)
            copy(peer, peer).wait_recv()
            return 0

        def sent(s, _):
            copy(me, lax.rem(me + s, n)).wait_send()
            return 0

        lax.fori_loop(1, n, send, 0)
        lax.fori_loop(1, n, receive, 0)
        total = lax.fori_loop(
            0, n, lambda p, acc: acc + red_in[p, 0:rows], jnp.zeros_like(value)
        )
        lax.fori_loop(1, n, sent, 0)
        return total

    half = k // 2
    lane = lax.broadcasted_iota(jnp.int32, (half, 2 * k), 1)

    def pack(doubled):
        return jnp.where(lane < k, doubled[:half], doubled[half:])

    def unpack(packed):
        return jnp.concatenate([packed, pltpu.roll(packed, k, 1)], axis=0)

    def inverse_factor(gram):
        sub = 8
        lanes = lax.broadcasted_iota(jnp.int32, (sub, 2 * k), 1)
        rows = lax.broadcasted_iota(jnp.int32, (sub, 2 * k), 0)
        sub_row = lax.broadcasted_iota(jnp.int32, (sub, 1), 0)
        parts = []
        for t in range(k // sub):
            unit = (lanes == rows + (t * sub + k)).astype(f32)
            parts.append(jnp.where(lanes < k, gram[t * sub : (t + 1) * sub], unit))
        for j in range(k):
            t0, r0 = divmod(j, sub)
            row = parts[t0][r0 : r0 + 1, :]
            scaled = row / row[:, j : j + 1]
            for t in range(t0, k // sub):
                column = parts[t][:, j : j + 1]
                if t == t0:
                    column = jnp.where(sub_row > r0, column, 0.0)
                parts[t] = parts[t] - column * scaled
        for t in range(k // sub):
            pivot = jnp.sum(
                jnp.where(lanes == rows + t * sub, parts[t], 0.0), axis=1, keepdims=True
            )
            parts[t] = parts[t] * lax.rsqrt(pivot)
        return pltpu.roll(jnp.concatenate(parts, axis=0), k, 1)[:, :k]

    def subspace_step(count, start, centre, last):
        def first_update(r, _):
            value = image[r] - centre * y_buf[start, r].astype(f32)
            y_buf[(start + 1) % 3, r] = value.astype(bf16)
            return 0

        over_blocks(first_update, 0)
        previous, current = start, (start + 1) % 3
        for _ in range(DEGREE - 1):
            operator(count, current)
            count += 1
            following = (current + 1) % 3

            def update(r, _, previous=previous, current=current, following=following):
                value = 2.0 * (applied(r) - centre * y_buf[current, r].astype(f32))
                value = value - y_buf[previous, r].astype(f32)
                y_buf[following, r] = value.astype(bf16)
                return 0

            over_blocks(update, 0)
            previous, current = current, following

        def gram_term(r, acc):
            block = y_buf[current, r]
            return acc + nt_dot(block, jnp.concatenate([block, block], axis=0))

        doubled = over_blocks(gram_term, jnp.zeros((k, 2 * k), f32))
        gram = unpack(reduce_sum(pack(doubled))) / total_rows
        inverse = inverse_factor(gram)
        high = inverse.astype(bf16)
        rest = inverse - high.astype(f32)
        middle = rest.astype(bf16)
        low = (rest - middle.astype(f32)).astype(bf16)
        left = jnp.concatenate([high, middle, low], axis=1)
        result = (current + 1) % 3

        def orthonormal(r, _):
            block = y_buf[current, r]
            stacked = jnp.concatenate([block, block, block], axis=0)
            y_buf[result, r] = jnp.dot(left, stacked, preferred_element_type=f32).astype(bf16)
            return 0

        over_blocks(orthonormal, 0)
        operator(count, result)
        count += 1
        if not last:

            def keep_image(r, acc):
                value = applied(r)
                image[r] = value
                return acc + value * y_buf[result, r].astype(f32)

            traced = over_blocks(keep_image, jnp.zeros((k, b), f32))
            traced = sum(traced[t * 8 : (t + 1) * 8] for t in range(k // 8))
            traced = reduce_sum(traced)
            traced = jnp.sum(jnp.sum(traced, axis=1, keepdims=True), axis=0, keepdims=True)
            return count, result, traced / total_rows

        def ritz_term(r, acc):
            value = applied(r)
            top = value.astype(bf16)
            bottom = (value - top.astype(f32)).astype(bf16)
            return acc + nt_dot(y_buf[result, r], jnp.concatenate([top, bottom], axis=0))

        doubled = over_blocks(ritz_term, jnp.zeros((k, 2 * k), f32))
        doubled = doubled + pltpu.roll(doubled, k, 1)
        ritz_ref[...] = unpack(reduce_sum(pack(doubled)))[:, :k] / total_rows
        for j in range(blocks):
            basis_ref[:, j * b : (j + 1) * b] = y_buf[result, j]
        return count, result, None

    operator(0, 0)

    def keep_first(r, _):
        image[r] = applied(r)
        return 0

    over_blocks(keep_first, 0)
    count, result, trace = subspace_step(1, 0, FIRST_CENTRE, False)
    subspace_step(count, result, trace / k - 1.0, True)


def sorted_order(keys):
    count = keys.shape[0]
    ids = jnp.arange(count)
    before = (keys[None, :] < keys[:, None]) | (
        (keys[None, :] == keys[:, None]) & (ids[None, :] < ids[:, None])
    )
    rank = jnp.sum(before.astype(jnp.int32), axis=1)
    return (rank[:, None] == ids[None, :]).astype(jnp.int32)


def place(onehot, values):
    return jnp.sum(onehot * values[:, None], axis=0).astype(jnp.int32)


def local(vectors, diag_tiles, pair_tiles, halo_tiles, halo_rows, pair_index, pair_count):
    n = lax.axis_size("dom")
    k, width = vectors.shape
    blocks, b = diag_tiles.shape[0], diag_tiles.shape[1]
    pairs = pair_tiles.shape[0]
    entries = blocks + 2 * pairs
    row_ids, col_ids = pair_index[0, :, 0], pair_index[0, :, 1]
    live = jnp.arange(pairs) < pair_count[0]
    block_ids = jnp.arange(blocks)
    pair_ids = jnp.arange(pairs)
    target = jnp.concatenate(
        [block_ids, jnp.where(live, row_ids, blocks), jnp.where(live, col_ids, blocks)]
    )
    source = jnp.concatenate([block_ids, col_ids, row_ids])
    tile = jnp.concatenate([block_ids, blocks + 2 * pair_ids + 1, blocks + 2 * pair_ids])
    onehot = sorted_order(target)
    tile_id, source_id = place(onehot, tile), place(onehot, source)
    keep = (tile_id >= blocks).astype(f32)
    end_of = jnp.sum((target[None, :] <= block_ids[:, None]).astype(jnp.int32), axis=1) - 1
    rows = halo_rows[0]
    halo_onehot = sorted_order(rows)
    halo_order = place(halo_onehot, jnp.arange(n))
    halo_sorted = place(halo_onehot, rows)
    halo_keep = jnp.concatenate(
        [jnp.zeros((1,), f32), (halo_sorted[1:] == halo_sorted[:-1]).astype(f32)]
    )
    upto = jnp.sum((rows[None, :] <= block_ids[:, None]).astype(jnp.int32), axis=1)
    halo_any = jnp.any(rows[None, :] == block_ids[:, None], axis=1).astype(f32)
    halo_end = jnp.maximum(upto - 1, 0)

    smem = pl.BlockSpec(memory_space=pltpu.SMEM)
    vmem = pl.BlockSpec(memory_space=pltpu.VMEM)
    hbm = pl.BlockSpec(memory_space=pl.ANY)
    return pl.pallas_call(
        functools.partial(kernel, n, float(width * n)),
        out_shape=(
            jax.ShapeDtypeStruct((k, width), bf16),
            jax.ShapeDtypeStruct((k, k), f32),
        ),
        in_specs=[smem] * 9 + [vmem, hbm, hbm, hbm],
        out_specs=(vmem, vmem),
        scratch_shapes=[
            pltpu.VMEM((entries, b, b), bf16),
            pltpu.VMEM((n, b, b), bf16),
            pltpu.VMEM((3, blocks, k, b), bf16),
            pltpu.VMEM((blocks, k, b), f32),
            pltpu.VMEM((entries, k, b), f32),
            pltpu.VMEM((n, k, b), f32),
            pltpu.VMEM((n, k, b), bf16),
            pltpu.VMEM((n, k, b), bf16),
            pltpu.VMEM((n, k, b), bf16),
            pltpu.VMEM((k // 2, 2 * k), f32),
            pltpu.VMEM((n, k // 2, 2 * k), f32),
            pltpu.SemaphoreType.DMA((3,)),
            pltpu.SemaphoreType.DMA((n,)),
            pltpu.SemaphoreType.DMA((2, n)),
            pltpu.SemaphoreType.DMA((n,)),
            pltpu.SemaphoreType.DMA((n,)),
        ],
        compiler_params=pltpu.CompilerParams(
            collective_id=0, has_side_effects=True, vmem_limit_bytes=48 * 1024 * 1024
        ),
    )(
        tile_id,
        source_id,
        keep,
        end_of,
        rows,
        halo_order,
        halo_keep,
        halo_end,
        halo_any,
        vectors,
        diag_tiles,
        pair_tiles.reshape(2 * pairs, b, b),
        halo_tiles,
    )


def solution(mesh):
    return jax.shard_map(
        local,
        mesh=mesh,
        in_specs=(
            P(None, "dom"),
            P("dom", None, None),
            P("dom", None, None, None),
            P("dom", None, None),
            P("dom", None),
            P("dom", None, None),
            P("dom"),
        ),
        out_specs=(P(None, "dom"), P()),
        check_vma=False,
    )
```

time: 510 us -> 214 us (0.42); the launches traced: 501 us -> 211 us
  Pallas kernels: 0 us -> 199 us
  matrix products: 165 us -> 0 us
  blocking collectives: 160 us -> 0 us
  local copies, waits for them, and re-layouts: 63.9 us -> 6.31 us
  starting transfers between devices: 51.3 us -> 0 us
  other arithmetic: 52.2 us -> 3.94 us
  waiting for transfers between devices: 5.72 us -> 0 us
    pallas_call x0 -> x1, Pallas kernels: none -> 199 us  [local(): pl.pallas_call(functools.partial(kernel, n, float(width * n)), out_shape=...]
    dot_general x69 -> x0, matrix products: 165 us -> none  [the longest x9 48 us: operator(): jnp.einsum('kej,eij->kei', from_cols, pair_tiles[:, 0], preferred_element...]
    psum x4 -> x0, blocking collectives: 160 us -> none  [the longest x2 78.6 us: subspace_step(): gram_matrix = lax.psum(partial_value, 'dom')]
    all_to_all x9 -> x0, starting transfers between devices: 51.3 us -> none  [operator(): lax.all_to_all(outgoing, 'dom', split_axis=1, concat_axis=1, tiled=True)]
    gather x27 -> x0, local copies, waits for them, and re-layouts: 47.3 us -> none  [the longest x9 17.7 us: operator(): from_cols = jnp.take(blocked, col_ids, axis=1)]
    another operation x10 -> x0, other arithmetic: 24.1 us -> none  [the longest x6 13 us: subspace_step(): chol_lower = jnp.linalg.cholesky(gram_matrix)]
    select_n x10 -> x1, other arithmetic: 17.3 us -> 0.76 us  [local(): jnp.where(live, row_ids, blocks)]
    unnamed x135 -> x10, local copies, waits for them, and re-layouts: 14.5 us -> 5.55 us
  transfers between devices with their start and end apart: 9 -> 0, of which waited for: 2 -> 0; matrix products, arithmetic and copies ran while one was open for 28% -> 0% of each run, Pallas kernels for 0% -> 0%
where the time goes in v1:
time: 214 us; the launch traced here: 211 us
  Pallas kernels  199 us (93%)
  local copies, waits for them, and re-layouts  6.31 us (3%)
  other arithmetic  3.94 us (2%)
    pallas_call x1, Pallas kernels, local(): pl.pallas_call(functools.partial(kernel, n, float(width * n)), out_shape=...  199 us
    unnamed x10, local copies, waits for them, and re-layouts  5.55 us

profile of v1, /device:TPU:0, one launch (start us, length us, event | category | flops | bytes accessed | tf_op | source)
XLA Modules:
  0.0 211.1 jit_solution(9932902605968345237)
XLA Ops:
  1.3 0.8 fusion.4
  2.1 0.8 compare_select_fusion.1
  2.8 0.9 convert_reduce_fusion.2
  3.8 0.7 select_reduce_fusion.2
  4.5 0.1 slice_compare_fusion
  4.6 0.1 add_convert_fusion.halo_keep
  4.7 0.8 slice_bitcast_fusion
  5.4 0.1 fusion.6
  5.5 0.1 convert_reduce_fusion.1
  5.6 0.2 convert_reduce_fusion
  5.8 0.2 select_reduce_fusion
  6.0 0.0 copy-start
  6.0 1.2 copy-done
  7.2 0.0 copy-start.1
  7.2 1.2 copy-done.1
  8.5 0.0 copy-start.2
  8.5 1.0 copy-done.2
  9.5 0.0 copy-start.3
  9.5 0.7 copy-done.3
  10.2 199.5 %shard_map.86 = (bf16[64,4096]{1,0:T(8,128)(2,1)S(1)}, f32[64,64]{1,0:T(8,128)S(1)}) custom-call(s32[224]{0:T(256)S(1)} %get-tuple-element.3.tile_id, s32[224]{0:T(256)S(1)} %get-tuple-element.2.source_id, f32[224]{0:T(256)S(1)} %compare_convert_fusion.keep, s32[32]{0:T(128)S(1)} %broadcast_add_fusion.end_of, s32[32]{0:T(128)S(1)} %bitcast.15, ...), custom_call_target="tpu_custom_call" | custom-call | tf_op jit(solution)/shard_map/pallas_call | solution.py:362
  209.7 0.8 copy.12
  210.4 0.6 copy.13
  (6 shorter events, 0.0 us)
Async XLA Ops:
  6.0 1.2 copy-start
  7.2 1.2 copy-start.1
  8.5 1.0 copy-start.2
  9.5 0.7 copy-start.3

commit v2 on v1

v2 whole, which is shorter than its diff:
```python
import functools

import jax
import jax.numpy as jnp
from jax import lax
from jax.experimental import pallas as pl
from jax.experimental.pallas import tpu as pltpu
from jax.sharding import PartitionSpec as P

DEGREE = 4
FIRST_CENTRE = -0.5
MESH = pl.DeviceIdType.MESH
f32 = jnp.float32
bf16 = jnp.bfloat16


def nt_dot(a, b):
    return lax.dot_general(a, b, (((1,), (1,)), ((), ())), preferred_element_type=f32)


def kernel(
    n,
    group,
    total_rows,
    ints,
    floats,
    vec_ref,
    diag_hbm,
    pair_hbm,
    halo_hbm,
    basis_ref,
    ritz_ref,
    tiles,
    halo_tiles,
    y_buf,
    image,
    partial,
    halo_part,
    halo_sum,
    stage,
    arrived_even,
    arrived_odd,
    far_out,
    near_out,
    far_in_a,
    near_in_a,
    far_in_b,
    near_in_b,
    load_sem,
    send_sem,
    recv_sem,
    far_send,
    near_send,
    far_recv,
    near_recv,
):
    me = lax.axis_index("dom")
    k, width = vec_ref.shape
    blocks = y_buf.shape[1]
    b = width // blocks
    entries = tiles.shape[0]
    pairs2 = entries - blocks
    groups = n // group
    bits = n.bit_length() - 1
    if n != 1 << bits:
        raise ValueError(n)
    flips = [(1 << t) * (1 - 2 * lax.rem(lax.div(me, 1 << t), 2)) for t in range(bits)]

    def partner(s):
        peer = me
        for t in range(bits):
            peer = peer + lax.rem(lax.div(s, 1 << t), 2) * flips[t]
        return peer

    at = 0

    def table(size):
        nonlocal at
        first = at
        at += size
        return lambda e: ints[first + e]

    tile_id, source_id, end_of = table(entries), table(entries), table(blocks)
    send_rows, halo_order, halo_end = table(n), table(n), table(blocks)

    def keep(e):
        return floats[e]

    def halo_keep(e):
        return floats[entries + e]

    def halo_any(r):
        return floats[entries + n + r]

    loads = [
        pltpu.make_async_copy(diag_hbm, tiles.at[pl.ds(0, blocks)], load_sem.at[0]),
        pltpu.make_async_copy(pair_hbm, tiles.at[pl.ds(blocks, pairs2)], load_sem.at[1]),
        pltpu.make_async_copy(halo_hbm, halo_tiles, load_sem.at[2]),
    ]
    for load in loads:
        load.start()

    barrier = pltpu.get_barrier_semaphore()

    def greet(s, _):
        pl.semaphore_signal(
            barrier, inc=1, device_id=(lax.rem(me + s, n),), device_id_type=MESH
        )
        return 0

    lax.fori_loop(1, n, greet, 0)
    for j in range(blocks):
        y_buf[0, j] = vec_ref[:, j * b : (j + 1) * b]
    pl.semaphore_wait(barrier, n - 1)

    slots = (arrived_even, arrived_odd)

    def halo_copy(slot, peer_from, peer_to):
        return pltpu.make_async_remote_copy(
            src_ref=stage.at[peer_to],
            dst_ref=slots[slot].at[peer_from],
            send_sem=send_sem.at[peer_to],
            recv_sem=recv_sem.at[slot, peer_from],
            device_id=(peer_to,),
            device_id_type=MESH,
        )

    entry_unroll = next(u for u in (8, 4, 2, 1) if entries % (2 * u) == 0)
    halo_unroll = next(u for u in (8, 4, 2, 1) if n % u == 0)
    near_unroll = min(4, halo_unroll)

    def no_hook():
        return None

    def operator(count, cur, early=no_hook, middle=no_hook, late=no_hook):
        slot = count % 2
        arrived = slots[slot]
        early()

        def send(i, _):
            peer = partner(n - 1 - i)
            stage[peer] = y_buf[cur, send_rows(peer)]
            halo_copy(slot, me, peer).start()
            return 0

        lax.fori_loop(0, n - 1, send, 0)
        arrived[me] = y_buf[cur, send_rows(me)]
        if count == 0:
            for load in loads:
                load.wait()

            def flip(p, _):
                halo_tiles[p] = halo_tiles[p].T
                return 0

            lax.fori_loop(0, n, flip, 0)

        def local(i, carry):
            for u in range(entry_unroll):
                e = i * entry_unroll + u
                product = jnp.dot(
                    y_buf[cur, source_id(e)], tiles[tile_id(e)], preferred_element_type=f32
                )
                carry = carry * keep(e) + product
                partial[e] = carry
            return carry

        steps = entries // entry_unroll
        carry = lax.fori_loop(0, steps // 2, local, jnp.zeros((k, b), f32))
        middle()
        lax.fori_loop(steps // 2, steps, local, carry)
        late()

        def arrivals(i, first):
            peers = [partner(i * near_unroll + u) for u in range(first, near_unroll)]
            for peer in peers:
                halo_copy(slot, peer, peer).wait_recv()
            if first:
                peers = [me] + peers
            products = [
                jnp.dot(arrived[peer], halo_tiles[peer], preferred_element_type=f32)
                for peer in peers
            ]
            for peer, product in zip(peers, products):
                halo_part[peer] = product
            return first

        arrivals(0, 1)
        lax.fori_loop(1, n // near_unroll, lambda i, x: arrivals(i, 0), 0)

        def halo(i, carry):
            for u in range(halo_unroll):
                e = i * halo_unroll + u
                carry = carry * halo_keep(e) + halo_part[halo_order(e)]
                halo_sum[e] = carry
            return carry

        lax.fori_loop(0, n // halo_unroll, halo, jnp.zeros((k, b), f32))

        def sent(s, _):
            halo_copy(slot, me, lax.rem(me + s, n)).wait_send()
            return 0

        lax.fori_loop(1, n, sent, 0)

    def applied(r):
        return partial[end_of(r)] + halo_sum[halo_end(r)] * halo_any(r)

    def over_blocks(body, init, unroll=4):
        def step(i, carry):
            for u in range(unroll):
                carry = body(i * unroll + u, carry)
            return carry

        if blocks % unroll:
            return lax.fori_loop(0, blocks, body, init)
        return lax.fori_loop(0, blocks // unroll, step, init)

    mine, team = lax.rem(me, group), lax.div(me, group)

    class Stage:
        def __init__(self, out, into, send_sems, recv_sems, size, place, device):
            self.out, self.into, self.size = out, into, size
            self.send_sems, self.recv_sems = send_sems, recv_sems
            self.place, self.device = place, device

        def copy(self, origin, other, rows):
            return pltpu.make_async_remote_copy(
                src_ref=self.out.at[pl.ds(0, rows)],
                dst_ref=self.into.at[origin, pl.ds(0, rows)],
                send_sem=self.send_sems.at[other],
                recv_sem=self.recv_sems.at[origin],
                device_id=(self.device(other),),
                device_id_type=MESH,
            )

        def start(self, value):
            rows = value.shape[0]
            self.out[0:rows] = value
            self.into[self.place, 0:rows] = value
            for s in range(1, self.size):
                self.copy(self.place, lax.rem(self.place + s, self.size), rows).start()

        def finish(self, rows):
            for s in range(1, self.size):
                other = lax.rem(self.place + s, self.size)
                self.copy(other, other, rows).wait_recv()
            total = self.into[0, 0:rows]
            for p in range(1, self.size):
                total = total + self.into[p, 0:rows]
            for s in range(1, self.size):
                self.copy(self.place, lax.rem(self.place + s, self.size), rows).wait_send()
            return total

    def two_stages(lane_set, far_in, near_in):
        far = Stage(
            far_out.at[lane_set],
            far_in,
            far_send.at[lane_set],
            far_recv.at[lane_set],
            groups,
            team,
            lambda other: other * group + mine,
        )
        near = Stage(
            near_out.at[lane_set],
            near_in,
            near_send.at[lane_set],
            near_recv.at[lane_set],
            group,
            mine,
            lambda other: team * group + other,
        )
        return far, near

    gram_stages = two_stages(0, far_in_a, near_in_a)
    other_stages = two_stages(1, far_in_b, near_in_b)

    half = k // 2
    lane = lax.broadcasted_iota(jnp.int32, (half, 2 * k), 1)

    def pack(doubled):
        return jnp.where(lane < k, doubled[:half], doubled[half:])

    def unpack(packed):
        return jnp.concatenate([packed, pltpu.roll(packed, k, 1)], axis=0)

    def inverse_factor(gram):
        sub = 8
        lanes = lax.broadcasted_iota(jnp.int32, (sub, 2 * k), 1)
        rows = lax.broadcasted_iota(jnp.int32, (sub, 2 * k), 0)
        sub_row = lax.broadcasted_iota(jnp.int32, (sub, 1), 0)
        parts = []
        for t in range(k // sub):
            unit = (lanes == rows + (t * sub + k)).astype(f32)
            parts.append(jnp.where(lanes < k, gram[t * sub : (t + 1) * sub], unit))
        for j in range(k):
            t0, r0 = divmod(j, sub)
            row = parts[t0][r0 : r0 + 1, :]
            scaled = row / row[:, j : j + 1]
            for t in range(t0, k // sub):
                column = parts[t][:, j : j + 1]
                if t == t0:
                    column = jnp.where(sub_row > r0, column, 0.0)
                parts[t] = parts[t] - column * scaled
        for t in range(k // sub):
            pivot = jnp.sum(
                jnp.where(lanes == rows + t * sub, parts[t], 0.0), axis=1, keepdims=True
            )
            parts[t] = parts[t] * lax.rsqrt(pivot)
        return pltpu.roll(jnp.concatenate(parts, axis=0), k, 1)[:, :k]

    def split(value):
        high = value.astype(bf16)
        rest = value - high.astype(f32)
        middle = rest.astype(bf16)
        return high, middle, (rest - middle.astype(f32)).astype(bf16)

    def recur(count, previous, current, following, centre):
        operator(count, current)

        def update(r, _):
            value = 2.0 * (applied(r) - centre * y_buf[current, r].astype(f32))
            value = value - y_buf[previous, r].astype(f32)
            y_buf[following, r] = value.astype(bf16)
            return 0

        over_blocks(update, 0)

    def orthonormal_image(count, current, result, visit, init):
        held = []

        def early():
            def gram_term(r, acc):
                block = y_buf[current, r]
                return acc + nt_dot(block, jnp.concatenate([block, block], axis=0))

            doubled = over_blocks(gram_term, jnp.zeros((k, 2 * k), f32))
            gram_stages[0].start(pack(doubled))

        def middle():
            gram_stages[1].start(gram_stages[0].finish(half))

        def late():
            gram = unpack(gram_stages[1].finish(half)) / total_rows
            held.extend(split(inverse_factor(gram)))

        operator(count, current, early, middle, late)
        w1, w2, w3 = held
        left = jnp.concatenate([w1, w2, w3], axis=1)
        left_image = jnp.concatenate([w1, w2, w3, w1, w2, w1], axis=1)

        def each(r, acc):
            block = y_buf[current, r]
            stacked = jnp.concatenate([block, block, block], axis=0)
            after = jnp.dot(left, stacked, preferred_element_type=f32).astype(bf16)
            y_buf[result, r] = after
            a1, a2, a3 = split(applied(r))
            right = jnp.concatenate([a1, a1, a1, a2, a2, a3], axis=0)
            return visit(r, after, jnp.dot(left_image, right, preferred_element_type=f32), acc)

        return over_blocks(each, init)

    operator(0, 0)

    def first_update(r, _):
        value = applied(r) - FIRST_CENTRE * y_buf[0, r].astype(f32)
        y_buf[1, r] = value.astype(bf16)
        return 0

    over_blocks(first_update, 0)
    count = 1
    order = [0, 1, 2]
    for _ in range(DEGREE - 1):
        recur(count, *order, FIRST_CENTRE)
        order = order[1:] + order[:1]
        count += 1
    current, result, rounded = order[1], order[2], order[0]

    def keep_image(r, after, value, acc):
        image[r] = value
        y_buf[rounded, r] = value.astype(bf16)
        return acc + value * after.astype(f32)

    traced = orthonormal_image(count, current, result, keep_image, jnp.zeros((k, b), f32))
    count += 1
    traced = sum(traced[t * 8 : (t + 1) * 8] for t in range(k // 8))
    held = []

    def trace_early():
        other_stages[0].start(traced)

    def trace_middle():
        other_stages[1].start(other_stages[0].finish(8))

    def trace_late():
        total = other_stages[1].finish(8)
        total = jnp.sum(jnp.sum(total, axis=1, keepdims=True), axis=0, keepdims=True)
        held.append(total / total_rows / k - 1.0)

    operator(count, rounded, trace_early, trace_middle, trace_late)
    count += 1
    centre = held[0]
    following = current

    def second_update(r, _):
        start = y_buf[result, r].astype(f32)
        first = image[r]
        value = first - centre * start
        y_buf[rounded, r] = value.astype(bf16)
        value = 2.0 * (applied(r) - centre * first - centre * value) - start
        y_buf[following, r] = value.astype(bf16)
        return 0

    over_blocks(second_update, 0)
    order = [rounded, following, result]
    for _ in range(DEGREE - 2):
        recur(count, *order, centre)
        order = order[1:] + order[:1]
        count += 1
    current, result = order[1], order[2]

    def ritz_term(r, after, value, acc):
        top = value.astype(bf16)
        bottom = (value - top.astype(f32)).astype(bf16)
        return acc + nt_dot(after, jnp.concatenate([top, bottom], axis=0))

    doubled = orthonormal_image(count, current, result, ritz_term, jnp.zeros((k, 2 * k), f32))
    doubled = doubled + pltpu.roll(doubled, k, 1)
    other_stages[0].start(pack(doubled))
    for j in range(blocks):
        basis_ref[:, j * b : (j + 1) * b] = y_buf[result, j]
    other_stages[1].start(other_stages[0].finish(half))
    ritz_ref[...] = unpack(other_stages[1].finish(half))[:, :k] / total_rows


def sorted_order(keys):
    count = keys.shape[0]
    ids = jnp.arange(count)
    before = (keys[None, :] < keys[:, None]) | (
        (keys[None, :] == keys[:, None]) & (ids[None, :] < ids[:, None])
    )
    rank = jnp.sum(before.astype(jnp.int32), axis=1)
    return (rank[:, None] == ids[None, :]).astype(jnp.int32)


def place(onehot, values):
    return jnp.sum(onehot * values[:, None], axis=0).astype(jnp.int32)


def local(vectors, diag_tiles, pair_tiles, halo_tiles, halo_rows, pair_index, pair_count):
    n = lax.axis_size("dom")
    k, width = vectors.shape
    blocks, b = diag_tiles.shape[0], diag_tiles.shape[1]
    pairs = pair_tiles.shape[0]
    entries = blocks + 2 * pairs
    row_ids, col_ids = pair_index[0, :, 0], pair_index[0, :, 1]
    live = jnp.arange(pairs) < pair_count[0]
    block_ids = jnp.arange(blocks)
    pair_ids = jnp.arange(pairs)
    target = jnp.concatenate(
        [block_ids, jnp.where(live, row_ids, blocks), jnp.where(live, col_ids, blocks)]
    )
    source = jnp.concatenate([block_ids, col_ids, row_ids])
    tile = jnp.concatenate([block_ids, blocks + 2 * pair_ids + 1, blocks + 2 * pair_ids])
    onehot = sorted_order(target)
    tile_id, source_id = place(onehot, tile), place(onehot, source)
    keep = (tile_id >= blocks).astype(f32)
    end_of = jnp.sum((target[None, :] <= block_ids[:, None]).astype(jnp.int32), axis=1) - 1
    rows = halo_rows[0]
    halo_onehot = sorted_order(rows)
    halo_order = place(halo_onehot, jnp.arange(n))
    halo_sorted = place(halo_onehot, rows)
    halo_keep = jnp.concatenate(
        [jnp.zeros((1,), f32), (halo_sorted[1:] == halo_sorted[:-1]).astype(f32)]
    )
    upto = jnp.sum((rows[None, :] <= block_ids[:, None]).astype(jnp.int32), axis=1)
    halo_any = jnp.any(rows[None, :] == block_ids[:, None], axis=1).astype(f32)
    halo_end = jnp.maximum(upto - 1, 0)

    ints = jnp.concatenate([tile_id, source_id, end_of, rows, halo_order, halo_end])
    floats = jnp.concatenate([keep, halo_keep, halo_any])
    group = next(g for g in (8, 4, 2, 1) if n % g == 0)
    piece = (k // 2, 2 * k)

    smem = pl.BlockSpec(memory_space=pltpu.SMEM)
    vmem = pl.BlockSpec(memory_space=pltpu.VMEM)
    hbm = pl.BlockSpec(memory_space=pl.ANY)
    return pl.pallas_call(
        functools.partial(kernel, n, group, float(width * n)),
        out_shape=(
            jax.ShapeDtypeStruct((k, width), bf16),
            jax.ShapeDtypeStruct((k, k), f32),
        ),
        in_specs=[smem] * 2 + [vmem, hbm, hbm, hbm],
        out_specs=(vmem, vmem),
        scratch_shapes=[
            pltpu.VMEM((entries, b, b), bf16),
            pltpu.VMEM((n, b, b), bf16),
            pltpu.VMEM((3, blocks, k, b), bf16),
            pltpu.VMEM((blocks, k, b), f32),
            pltpu.VMEM((entries, k, b), f32),
            pltpu.VMEM((n, k, b), f32),
            pltpu.VMEM((n, k, b), f32),
            pltpu.VMEM((n, k, b), bf16),
            pltpu.VMEM((n, k, b), bf16),
            pltpu.VMEM((n, k, b), bf16),
            pltpu.VMEM((2, *piece), f32),
            pltpu.VMEM((2, *piece), f32),
            pltpu.VMEM((n // group, *piece), f32),
            pltpu.VMEM((group, *piece), f32),
            pltpu.VMEM((n // group, *piece), f32),
            pltpu.VMEM((group, *piece), f32),
            pltpu.SemaphoreType.DMA((3,)),
            pltpu.SemaphoreType.DMA((n,)),
            pltpu.SemaphoreType.DMA((2, n)),
            pltpu.SemaphoreType.DMA((2, n // group)),
            pltpu.SemaphoreType.DMA((2, group)),
            pltpu.SemaphoreType.DMA((2, n // group)),
            pltpu.SemaphoreType.DMA((2, group)),
        ],
        compiler_params=pltpu.CompilerParams(
            collective_id=0, has_side_effects=True, vmem_limit_bytes=48 * 1024 * 1024
        ),
    )(
        ints,
        floats,
        vectors,
        diag_tiles,
        pair_tiles.reshape(2 * pairs, b, b),
        halo_tiles,
    )


def solution(mesh):
    return jax.shard_map(
        local,
        mesh=mesh,
        in_specs=(
            P(None, "dom"),
            P("dom", None, None),
            P("dom", None, None, None),
            P("dom", None, None),
            P("dom", None),
            P("dom", None, None),
            P("dom"),
        ),
        out_specs=(P(None, "dom"), P()),
        check_vma=False,
    )
```

time: 214 us -> 174 us (0.81); the launches traced: 211 us -> 174 us
  Pallas kernels: 199 us -> 162 us
    pallas_call x1, Pallas kernels: 199 us -> 162 us  [local(): pl.pallas_call(functools.partial(kernel, n, group, float(width * n)), out...]
    unnamed x10 -> x8, local copies, waits for them, and re-layouts: 5.55 us -> 4.91 us
where the time goes in v2:
time: 174 us
  Pallas kernels  162 us (93%)
  local copies, waits for them, and re-layouts  6.4 us (4%)
  other arithmetic  4.11 us (2%)
    pallas_call x1, Pallas kernels, local(): pl.pallas_call(functools.partial(kernel, n, group, float(width * n)), out...  162 us
    unnamed x8, local copies, waits for them, and re-layouts  4.91 us

profile of v2, /device:TPU:0, one launch (start us, length us, event | category | flops | bytes accessed | tf_op | source)
XLA Modules:
  0.0 173.6 jit_solution(310540432765550925)
XLA Ops:
  1.3 0.9 convert_reduce_fusion.3
  2.2 0.8 fusion.4
  3.0 0.9 select_reduce_fusion.2
  3.9 0.1 slice_compare_fusion
  4.0 0.8 compare_select_fusion.1
  4.8 0.8 slice_bitcast_fusion
  5.5 0.1 fusion.6
  5.6 0.1 convert_reduce_fusion.1
  5.7 0.2 convert_reduce_fusion
  5.9 0.2 select_reduce_fusion
  6.1 0.7 concatenate.20.ints
  6.8 0.1 add_convert_fusion.floats
  6.9 0.0 copy-start
  6.9 1.2 copy-done
  8.1 0.0 copy-start.1
  8.1 1.2 copy-done.1
  9.4 0.0 copy-start.2
  9.4 1.0 copy-done.2
  10.4 161.8 %shard_map.86 = (bf16[64,4096]{1,0:T(8,128)(2,1)S(1)}, f32[64,64]{1,0:T(8,128)S(1)}) custom-call(s32[576]{0:T(1024)S(1)} %concatenate.20.ints, f32[288]{0:T(512)S(1)} %add_convert_fusion.floats, bf16[64,4096]{1,0:T(8,128)(2,1)S(1)} %copy-done.2, bf16[32,128,128]{2,1,0:T(8,128)(2,1)S(1)} %copy-done, bf16[192,128,128]{2,1,0:T(8,128)(2,1)} %bitcast.12, ...), custom_call_target="tpu_custom_call" | custom-call | tf_op jit(solution)/shard_map/pallas_call | solution.py:489
  172.2 0.8 copy.12
  173.0 0.6 copy.13
  (5 shorter events, 0.0 us)
Async XLA Ops:
  6.9 1.2 copy-start
  8.1 1.2 copy-start.1
  9.4 1.0 copy-start.2

commit v3 on v2

--- a/solution.py
+++ b/solution.py
@@ -66,11 +66,21 @@
         raise ValueError(n)
     flips = [(1 << t) * (1 - 2 * lax.rem(lax.div(me, 1 << t), 2)) for t in range(bits)]
 
-    def partner(s):
-        peer = me
-        for t in range(bits):
-            peer = peer + lax.rem(lax.div(s, 1 << t), 2) * flips[t]
-        return peer
+    low_bits = min(3, bits)
+    chunk = 1 << low_bits
+
+    def partners(high, lows):
+        base = me
+        if not isinstance(high, int) or high:
+            for t in range(low_bits, bits):
+                scaled = lax.div(high, 1 << (t - low_bits))
+                base = base + lax.rem(scaled, 2) * flips[t]
+        for low in lows:
+            peer = base
+            for t in range(low_bits):
+                if low >> t & 1:
+                    peer = peer + flips[t]
+            yield high * chunk + low, peer
 
     at = 0
 
@@ -115,19 +125,18 @@
 
     slots = (arrived_even, arrived_odd)
 
-    def halo_copy(slot, peer_from, peer_to):
+    def halo_copy(slot, s, peer):
         return pltpu.make_async_remote_copy(
-            src_ref=stage.at[peer_to],
-            dst_ref=slots[slot].at[peer_from],
-            send_sem=send_sem.at[peer_to],
-            recv_sem=recv_sem.at[slot, peer_from],
-            device_id=(peer_to,),
+            src_ref=stage.at[s],
+            dst_ref=slots[slot].at[s],
+            send_sem=send_sem.at[s],
+            recv_sem=recv_sem.at[slot, s],
+            device_id=(peer,),
             device_id_type=MESH,
         )
 
     entry_unroll = next(u for u in (8, 4, 2, 1) if entries % (2 * u) == 0)
     halo_unroll = next(u for u in (8, 4, 2, 1) if n % u == 0)
-    near_unroll = min(4, halo_unroll)
 
     def no_hook():
         return None
@@ -137,14 +146,18 @@
         arrived = slots[slot]
         early()
 
-        def send(i, _):
-            peer = partner(n - 1 - i)
-            stage[peer] = y_buf[cur, send_rows(peer)]
-            halo_copy(slot, me, peer).start()
+        def send(high, first):
+            for s, peer in partners(high, range(chunk - 1, first - 1, -1)):
+                stage[s] = y_buf[cur, send_rows(peer)]
+                halo_copy(slot, s, peer).start()
+
+        def send_high(i, _):
+            send(n // chunk - 1 - i, 0)
             return 0
 
-        lax.fori_loop(0, n - 1, send, 0)
-        arrived[me] = y_buf[cur, send_rows(me)]
+        lax.fori_loop(0, n // chunk - 1, send_high, 0)
+        send(0, 1)
+        arrived[0] = y_buf[cur, send_rows(me)]
         if count == 0:
             for load in loads:
                 load.wait()
@@ -171,22 +184,21 @@
         lax.fori_loop(steps // 2, steps, local, carry)
         late()
 
-        def arrivals(i, first):
-            peers = [partner(i * near_unroll + u) for u in range(first, near_unroll)]
-            for peer in peers:
-                halo_copy(slot, peer, peer).wait_recv()
-            if first:
-                peers = [me] + peers
-            products = [
-                jnp.dot(arrived[peer], halo_tiles[peer], preferred_element_type=f32)
-                for peer in peers
-            ]
-            for peer, product in zip(peers, products):
-                halo_part[peer] = product
-            return first
+        def arrivals(high, first):
+            steps = list(partners(high, range(chunk)))
+            for s, peer in steps[first:]:
+                halo_copy(slot, s, peer).wait_recv()
+            for s, peer in steps:
+                halo_part[peer] = jnp.dot(
+                    arrived[s], halo_tiles[peer], preferred_element_type=f32
+                )
+
+        def arrivals_high(i, _):
+            arrivals(i, 0)
+            return 0
 
         arrivals(0, 1)
-        lax.fori_loop(1, n // near_unroll, lambda i, x: arrivals(i, 0), 0)
+        lax.fori_loop(1, n // chunk, arrivals_high, 0)
 
         def halo(i, carry):
             for u in range(halo_unroll):
@@ -197,11 +209,8 @@
 
         lax.fori_loop(0, n // halo_unroll, halo, jnp.zeros((k, b), f32))
 
-        def sent(s, _):
-            halo_copy(slot, me, lax.rem(me + s, n)).wait_send()
-            return 0
-
-        lax.fori_loop(1, n, sent, 0)
+        for s in range(1, n):
+            halo_copy(slot, s, me + flips[0]).wait_send()
 
     def applied(r):
         return partial[end_of(r)] + halo_sum[halo_end(r)] * halo_any(r)
@@ -520,7 +529,7 @@
             pltpu.SemaphoreType.DMA((2, group)),
         ],
         compiler_params=pltpu.CompilerParams(
-            collective_id=0, has_side_effects=True, vmem_limit_bytes=48 * 1024 * 1024
+            collective_id=0, has_side_effects=True, vmem_limit_bytes=60 * 1024 * 1024
         ),
     )(
         ints,

time: 174 us -> 167 us (0.960)
  Pallas kernels: 162 us -> 156 us
    pallas_call x1, Pallas kernels: 162 us -> 156 us  [local(): pl.pallas_call(functools.partial(kernel, n, group, float(width * n)), out...]
    unnamed x8 -> x2, local copies, waits for them, and re-layouts: 4.91 us -> 3.24 us
where the time goes in v3:
time: 167 us
  Pallas kernels  156 us (93%)
  local copies, waits for them, and re-layouts  5.33 us (3%)
  other arithmetic  4.69 us (3%)
    pallas_call x1, Pallas kernels, local(): pl.pallas_call(functools.partial(kernel, n, group, float(width * n)), out...  156 us

profile of v3, /device:TPU:0, one launch (start us, length us, event | category | flops | bytes accessed | tf_op | source)
XLA Modules:
  0.0 166.9 jit_solution(12133964338195742898)
XLA Ops:
  1.3 0.9 convert_reduce_fusion.3
  2.2 0.8 fusion.4
  3.0 0.9 select_reduce_fusion.2
  3.9 0.1 slice_compare_fusion
  4.0 0.8 compare_select_fusion.1
  4.8 0.8 slice_bitcast_fusion
  5.5 0.1 fusion.6
  5.6 0.1 convert_reduce_fusion.1
  5.7 0.2 convert_reduce_fusion
  5.9 0.2 select_reduce_fusion
  6.1 1.3 concatenate.20.ints
  7.4 0.7 add_convert_fusion.floats
  8.1 155.5 %shard_map.86 = (bf16[64,4096]{1,0:T(8,128)(2,1)}, f32[64,64]{1,0:T(8,128)}) custom-call(s32[576]{0:T(1024)} %concatenate.20.ints, f32[288]{0:T(512)} %add_convert_fusion.floats, bf16[64,4096]{1,0:T(8,128)(2,1)} %vec_ref.1, bf16[32,128,128]{2,1,0:T(8,128)(2,1)} %diag_hbm.1, bf16[192,128,128]{2,1,0:T(8,128)(2,1)} %bitcast.12, bf16[32,128,128]{2,1,0:T(8,128)(2,1)} %halo_hbm.1), custom_call_target="tpu_custom_call" | custom-call | tf_op jit(solution)/shard_map/pallas_call | solution.py:498
  163.6 1.9 %copy.12 = bf16[64,4096]{1,0:T(8,128)(2,1)} copy(bf16[64,4096]{1,0:T(8,128)(2,1)} %get-tuple-element.17) | data formatting | bytes 1048576
  165.5 1.4 copy.13
  (5 shorter events, 0.0 us)
